TPU v7x, 256 devices: a whole 4x4x8 slice. The times are simulated.
256 devices in a mesh: seq: 16 (over z, core), pipe: 4 (over y), dp: 4 (over x).
Axes of the slice: x: 4, y: 4, z: 8, core: 2. Of those that a mesh axis runs over, the one named last changes fastest.
Arguments:
- segment_input: bfloat16 [4, 4096, 3072], P('pipe', ('dp', 'seq')), parts along dimension 1
- output_grad: bfloat16 [4, 4096, 3072], P('pipe', ('dp', 'seq')), parts along dimension 1, may hold values from -6 to 6
- qkv_weight: bfloat16 [4, 3072, 16, 384], P('pipe', None, 'seq')
- out_weight: bfloat16 [4, 2048, 3072], P('pipe', 'seq'), may hold values from -0.125 to 0.125
- query_gain: float32 [4, 128], P('pipe')
- key_gain: float32 [4, 128], P('pipe')
- gate_scale: float32 [4, 3072], P('pipe'), may hold values from -4 to 4
- neighbours: int32 [64, 27], P('dp'), parts along dimension 0, may hold values from -1 to 15
- tile_slot: int32 [64], P('dp'), parts along dimension 0, may hold values from 0 to 15, as said below
Outputs:
- segment_output: bfloat16 [4, 4096, 3072], P('pipe', ('dp', 'seq')), parts along dimension 1
- input_grad: bfloat16 [4, 4096, 3072], P('pipe', ('dp', 'seq')), parts along dimension 1
- gate_grad: float32 [16, 3072], P(('dp', 'pipe'), 'seq'), parts along dimension 0
There are 4 independent parts, one for each index of `dp`. A program takes and returns all parts, laid end to end along the dimension named above; an argument that names none is the same for every part. Nothing has to cross between parts.
Inputs may be any that keep to these rules, and one draw needn't show every extreme that they name: `tile_slot`: A permutation of 0 to 15.
All inputs are finite; a program needn't handle non-finite values.
Results may differ from a plain program's by a relative error of at most 0.02.
Values may be sent and summed in bfloat16 or wider, within the bound.
A program may use at most 128 MiB of HBM per device.

v0:
```python
import math
import jax
import jax.numpy as jnp
from jax import lax
from jax.sharding import PartitionSpec as P

TILE = 64
EPSILON = 1e-06


def passed_along(block, axis, distance):
    devices = range(lax.axis_size(axis))
    route = [((i - distance) % len(devices), i) for i in devices]
    return lax.ppermute(block, axis, route)


def slot_lists(neighbours, tile_slot):
    tile_count = tile_slot.shape[0]
    numbering = jnp.arange(tile_count, dtype=jnp.int32)
    placed = (tile_slot[:, None] == numbering[None, :]).astype(jnp.int32)
    tile_of_slot = jnp.sum(placed * numbering[:, None], axis=0)
    chosen = (tile_of_slot[:, None] == numbering[None, :]).astype(jnp.int32)
    listed_tiles = jnp.sum(chosen[:, :, None] * neighbours[None, :, :], axis=1)
    key_valid = listed_tiles >= 0
    safe_tiles = jnp.maximum(listed_tiles, 0)
    matches = (safe_tiles[:, :, None] == numbering[None, None, :]).astype(jnp.int32)
    key_slots = jnp.sum(matches * tile_slot[None, None, :], axis=2)
    return (key_slots, key_valid)


def block_tiles(tile_count):
    return math.gcd(tile_count, max(1, 512 // TILE))


def unit_norm(values):
    spread = jnp.sqrt(jnp.mean(values * values, axis=-1, keepdims=True) + EPSILON)
    return (values / spread, spread)


def probabilities(query_block, key_rows, block_valid):
    scores = jnp.einsum(
        "aihd,ajhd->ahij", query_block, key_rows, preferred_element_type=jnp.float32
    ) * (1.0 / math.sqrt(query_block.shape[-1]))
    key_mask = jnp.repeat(block_valid, TILE, axis=1)
    scores = jnp.where(key_mask[:, None, None, :], scores, -jnp.inf)
    row_max = jnp.max(scores, axis=-1, keepdims=True)
    weights = jnp.exp(scores - row_max)
    return (weights / jnp.sum(weights, axis=-1, keepdims=True)).astype(jnp.bfloat16)


def gathered(tiles_array, block_slots):
    picked = tiles_array[block_slots]
    return picked.reshape(block_slots.shape[0], -1, tiles_array.shape[2], tiles_array.shape[3])


def attend_both(query_tiles, key_tiles, value_tiles, grad_tiles, key_slots, key_valid):
    tile_count = query_tiles.shape[0]
    span = block_tiles(tile_count)
    scale_factor = 1.0 / math.sqrt(query_tiles.shape[-1])
    empty_grad = jnp.zeros(query_tiles.shape, jnp.float32)

    def per_block(accumulators, block_index):
        key_total, value_total = accumulators
        first_tile = block_index * span
        query_block = lax.dynamic_slice_in_dim(query_tiles, first_tile, span, 0)
        grad_block = lax.dynamic_slice_in_dim(grad_tiles, first_tile, span, 0)
        block_slots = lax.dynamic_slice_in_dim(key_slots, first_tile, span, 0)
        block_valid = lax.dynamic_slice_in_dim(key_valid, first_tile, span, 0)
        key_rows = gathered(key_tiles, block_slots)
        value_rows = gathered(value_tiles, block_slots)
        weights = probabilities(query_block, key_rows, block_valid)
        attended = jnp.einsum(
            "ahij,ajhd->aihd", weights, value_rows, preferred_element_type=jnp.float32
        )
        value_part = jnp.einsum(
            "ahij,aihd->ajhd", weights, grad_block, preferred_element_type=jnp.float32
        )
        prob_grad = jnp.einsum(
            "aihd,ajhd->ahij", grad_block, value_rows, preferred_element_type=jnp.float32
        )
        weights_wide = weights.astype(jnp.float32)
        row_delta = jnp.sum(weights_wide * prob_grad, axis=-1, keepdims=True)
        score_grad = (weights_wide * (prob_grad - row_delta) * scale_factor).astype(jnp.bfloat16)
        query_part = jnp.einsum(
            "ahij,ajhd->aihd", score_grad, key_rows, preferred_element_type=jnp.float32
        )
        key_part = jnp.einsum(
            "ahij,aihd->ajhd", score_grad, query_block, preferred_element_type=jnp.float32
        )
        block_shape = (span, block_slots.shape[1]) + query_tiles.shape[1:]
        key_total = key_total.at[block_slots].add(key_part.reshape(block_shape))
        value_total = value_total.at[block_slots].add(value_part.reshape(block_shape))
        return ((key_total, value_total), (attended, query_part))

    totals, parts = lax.scan(
        per_block, (empty_grad, empty_grad), jnp.arange(tile_count // span, dtype=jnp.int32)
    )
    flat_shape = (-1,) + query_tiles.shape[2:]
    return (
        parts[0].reshape(flat_shape),
        parts[1].reshape(flat_shape),
        totals[0].reshape(flat_shape),
        totals[1].reshape(flat_shape),
    )


def body(
    segment_input,
    output_grad,
    qkv_weight,
    out_weight,
    query_gain,
    key_gain,
    gate_scale,
    neighbours,
    tile_slot,
):
    key_slots, key_valid = slot_lists(neighbours, tile_slot)
    stream = segment_input[0]
    upstream = output_grad[0]
    model_width = stream.shape[1]
    head_dim = query_gain.shape[1]
    local_heads = qkv_weight.shape[2]
    local_width = local_heads * head_dim
    proj_weight = qkv_weight[0].reshape(model_width, local_heads * 3 * head_dim)
    out_local = out_weight[0]
    gate_row = gate_scale[0]
    query_weights = query_gain[0]
    key_weights = key_gain[0]
    projected = jnp.dot(
        lax.all_gather(stream, "seq", axis=0, tiled=True),
        proj_weight,
        preferred_element_type=jnp.float32,
    )
    all_tokens = projected.shape[0]
    projected = projected.reshape(all_tokens, local_heads, 3, head_dim)
    query_unit, query_spread = unit_norm(projected[:, :, 0])
    key_unit, key_spread = unit_norm(projected[:, :, 1])
    queries = (query_unit * query_weights).astype(jnp.bfloat16)
    keys_normed = (key_unit * key_weights).astype(jnp.bfloat16)
    value_rows = projected[:, :, 2].astype(jnp.bfloat16)
    scaled = (upstream.astype(jnp.float32) * gate_row).astype(jnp.bfloat16)
    attended_grad = jnp.einsum(
        "td,cd->tc",
        lax.all_gather(scaled, "seq", axis=0, tiled=True),
        out_local,
        preferred_element_type=jnp.float32,
    ).astype(jnp.bfloat16)

    def as_tiles(values):
        return values.reshape(-1, TILE, local_heads, head_dim)

    attended, query_grad, key_grad, value_grad = attend_both(
        as_tiles(queries),
        as_tiles(keys_normed),
        as_tiles(value_rows),
        as_tiles(attended_grad),
        key_slots,
        key_valid,
    )
    attended_low = attended.astype(jnp.bfloat16).reshape(all_tokens, local_width)
    rows = attended_low
    attention_out = lax.psum_scatter(
        jnp.dot(rows, out_local, preferred_element_type=jnp.float32),
        "seq",
        scatter_dimension=0,
        tiled=True,
    )
    section_out = (stream.astype(jnp.float32) + gate_row * attention_out).astype(jnp.bfloat16)
    segment_output = passed_along(section_out, "pipe", 1)
    gate_local = lax.psum_scatter(
        jnp.sum(upstream.astype(jnp.float32) * attention_out, axis=0),
        "seq",
        scatter_dimension=0,
        tiled=True,
    )
    query_scaled = query_grad * query_weights
    query_part_grad = (
        query_scaled - query_unit * jnp.mean(query_scaled * query_unit, axis=-1, keepdims=True)
    ) / query_spread
    key_scaled = key_grad * key_weights
    key_part_grad = (
        key_scaled - key_unit * jnp.mean(key_scaled * key_unit, axis=-1, keepdims=True)
    ) / key_spread
    projected_grad = (
        jnp.stack([query_part_grad, key_part_grad, value_grad], axis=2)
        .astype(jnp.bfloat16)
        .reshape(all_tokens, local_heads * 3 * head_dim)
    )
    rows = projected_grad
    stream_grad = lax.psum_scatter(
        jnp.einsum("tc,dc->td", rows, proj_weight, preferred_element_type=jnp.float32).astype(
            jnp.bfloat16
        ),
        "seq",
        scatter_dimension=0,
        tiled=True,
    ).astype(jnp.float32)
    token_grad = (upstream.astype(jnp.float32) + stream_grad).astype(jnp.bfloat16)
    input_grad = passed_along(token_grad, "pipe", -1)
    return (segment_output[None], input_grad[None], gate_local[None])


def solution(mesh):
    in_specs = (
        P("pipe", ("dp", "seq"), None),
        P("pipe", ("dp", "seq"), None),
        P("pipe", None, "seq", None),
        P("pipe", "seq", None),
        P("pipe", None),
        P("pipe", None),
        P("pipe", None),
        P("dp", None),
        P("dp"),
    )
    out_specs = (
        P("pipe", ("dp", "seq"), None),
        P("pipe", ("dp", "seq"), None),
        P(("dp", "pipe"), "seq"),
    )
    return jax.shard_map(body, mesh=mesh, in_specs=in_specs, out_specs=out_specs, check_vma=False)
```

profile of v0, /device:TPU:2, one launch (start us, length us, event | category | flops | bytes accessed | tf_op | source)
XLA Modules:
  0.0 510.5 jit_solution(14000528992266416604)
XLA Ops:
  9.9 2.8 copy.22
  13.2 45.7 %all-gather.6.cloned.1.call-done = bf16[1,1024,3072]{2,1,0:T(8,128)(2,1)} async-done(((bf16[1,64,3072]{2,1,0:T(8,128)(2,1)}), bf16[1,1024,3072]{2,1,0:T(8,128)(2,1)}) %all-gather.6.cloned.1.call-update) | async-done | bytes 6291472 | tf_op jit(solution)/shard_map/all_gather | solution.py:131
  58.9 5.5 %fusion.43 = f32[1024,1,3,128]{3,0,2,1:T(8,128)S(1)} fusion(bf16[3,128,3072]{2,1,0:T(8,128)(2,1)S(1)} %bitcast.180, bf16[1,1024,3072]{2,1,0:T(8,128)(2,1)} %all-gather.6.cloned.1.call-done), kind=kOutput, calls=%fused_computation.52 | convolution fusion | flops 2415919104 | bytes 10223616 | tf_op jit(solution)/shard_map/dot_general | solution.py:130
  67.4 38.6 %all-gather.4.cloned.1.call-done = bf16[1024,3072]{1,0:T(8,128)(2,1)} async-done(((bf16[64,3072]{1,0:T(8,128)(2,1)}), bf16[1024,3072]{1,0:T(8,128)(2,1)}) %all-gather.4.cloned.1.call-update) | async-done | bytes 6291472 | tf_op jit(solution)/shard_map/all_gather | solution.py:145
  106.0 4.6 convolution_convert_fusion.1
  110.8 179.4 %while.16 = (s32[]{:T(128)}, f32[16,64,1,128]{3,1,0,2:T(8,128)S(1)}, f32[16,64,1,128]{3,1,0,2:T(8,128)S(1)}, bf16[2,8,64,1,128]{4,2,1,3,0:T(8,128)(2,1)}, f32[2,...) while((s32[]{:T(128)}, ...), condition=%wide.region_11.12_spmd, body=%wide.region_5.11_spmd.sunk | while | flops 1380196096 | bytes 147397712 | solution.py:95
  112.6 2.9 gather_fusion.1
  115.5 2.9 gather_fusion
  118.4 5.3 %exponential_reduce_fusion.2 = (f32[8,64]{1,0:T(8,128)S(1)}, f32[8,64,1728]{2,1,0:T(8,128)}) fusion(bf16[8,1728,128]{2,1,0:T(8,128)(2,1)} %bitcast.173, pred[8,1728]{1,0:T(8,128)(4,1)S(1)} %broadcast_in_dim.84, bf16[16,64,1,128]{3,1,0,2:T(8,128)(2,1)S(1)} %get-tuple-element.237, s32[]{:T(128)S(6)} %select_n.30), kind=kOutput, calls=%fused_computation.13.clone.1 | convolution fusion | flops 230033088 | bytes 7225348 | tf_op jit(solution)/shard_map/while/body/eval_jaxpr/sub | solution.py:47
  123.7 2.8 divide_convert_fusion.3
  129.3 3.2 fusion.94
  132.5 7.1 %fusion.98 = f32[2,8,64,1,128]{4,2,1,3,0:T(8,128)} fusion(f32[2,8,64,1,128]{4,2,1,3,0:T(8,128)} %get-tuple-element.218, s32[]{:T(128)S(6)} %copy.34, bf16[8,1728,128]{2,1,0:T(8,128)(2,1)} %bitcast.174, bf16[8,64,1728]{2,1,0:T(8,128)(2,1)} %copy-done.2, f32[8,64,1728]{2,1,0:T(8,128)} %fusion.94), kind=kOutput, calls=%fused_computation.20.clone.1 | convolution fusion | flops 232687808 | bytes 14811140 | tf_op jit(solution)/shard_map/while/body/eval_jaxpr/ahij,ajhd->aihd/dot_general | solution.py:84
  139.6 8.8 %fusion.95 = f32[8,128,1728]{1,2,0:T(8,128)} fusion(bf16[8,64,1728]{2,1,0:T(8,128)(2,1)} %copy-done.2, f32[8,64,1728]{2,1,0:T(8,128)} %fusion.94, bf16[16,64,1,128]{3,1,0,2:T(8,128)(2,1)S(1)} %get-tuple-element.237, s32[]{:T(128)S(6)} %select_n.30), kind=kOutput, calls=%fused_computation.16.clone.1 | convolution fusion | flops 232687808 | bytes 18219012 | tf_op jit(solution)/shard_map/while/body/eval_jaxpr/ahij,aihd->ajhd/dot_general | solution.py:87
  148.4 23.2 %scatter_fusion = f32[16,64,128]{2,1,0:T(8,128)S(1)} fusion(f32[16,64,128]{2,1,0:T(8,128)S(1)} %bitcast.162, s32[216]{0:T(256)S(1)} %reshape.617, f32[216,64,128]{2,1,0:T(8,128)} %bitcast.172), kind=kCustom, calls=%fused_computation.2.clone.1 | custom fusion | flops 1769472 | bytes 21234528 | tf_op jit(solution)/shard_map/while/body/eval_jaxpr/scatter-add | solution.py:91
  171.6 5.7 %fusion.96 = f32[8,128,1728]{1,2,0:T(8,128)} fusion(bf16[8,64,1728]{2,1,0:T(8,128)(2,1)} %copy-done.2, bf16[16,64,1,128]{3,1,0,2:T(8,128)(2,1)S(1)} %get-tuple-element.240, s32[]{:T(128)S(6)} %select_n.30), kind=kOutput, calls=%fused_computation.23.clone.1 | convolution fusion | flops 226492416 | bytes 8978436 | tf_op jit(solution)/shard_map/while/body/eval_jaxpr/ahij,aihd->ajhd/dot_general | solution.py:75
  177.3 23.2 %scatter_fusion.1 = f32[16,64,128]{2,1,0:T(8,128)S(1)} fusion(f32[16,64,128]{2,1,0:T(8,128)S(1)} %bitcast.164, s32[216]{0:T(256)S(1)} %reshape.617, f32[216,64,128]{2,1,0:T(8,128)} %bitcast.171), kind=kCustom, calls=%fused_computation.3.clone.1 | custom fusion | flops 1769472 | bytes 21234528 | tf_op jit(solution)/shard_map/while/body/eval_jaxpr/scatter-add | solution.py:92
  202.2 2.9 gather_fusion.1
  205.0 2.9 gather_fusion
  208.0 5.3 %exponential_reduce_fusion.2 = (f32[8,64]{1,0:T(8,128)S(1)}, f32[8,64,1728]{2,1,0:T(8,128)}) fusion(bf16[8,1728,128]{2,1,0:T(8,128)(2,1)} %bitcast.173, pred[8,1728]{1,0:T(8,128)(4,1)S(1)} %broadcast_in_dim.84, bf16[16,64,1,128]{3,1,0,2:T(8,128)(2,1)S(1)} %get-tuple-element.237, s32[]{:T(128)S(6)} %select_n.30), kind=kOutput, calls=%fused_computation.13.clone.1 | convolution fusion | flops 230033088 | bytes 7225348 | tf_op jit(solution)/shard_map/while/body/eval_jaxpr/sub | solution.py:47
  213.3 2.8 divide_convert_fusion.3
  218.9 3.2 fusion.94
  222.1 7.1 %fusion.98 = f32[2,8,64,1,128]{4,2,1,3,0:T(8,128)} fusion(f32[2,8,64,1,128]{4,2,1,3,0:T(8,128)} %get-tuple-element.218, s32[]{:T(128)S(6)} %copy.34, bf16[8,1728,128]{2,1,0:T(8,128)(2,1)} %bitcast.174, bf16[8,64,1728]{2,1,0:T(8,128)(2,1)} %copy-done.2, f32[8,64,1728]{2,1,0:T(8,128)} %fusion.94), kind=kOutput, calls=%fused_computation.20.clone.1 | convolution fusion | flops 232687808 | bytes 14811140 | tf_op jit(solution)/shard_map/while/body/eval_jaxpr/ahij,ajhd->aihd/dot_general | solution.py:84
  229.2 8.8 %fusion.95 = f32[8,128,1728]{1,2,0:T(8,128)} fusion(bf16[8,64,1728]{2,1,0:T(8,128)(2,1)} %copy-done.2, f32[8,64,1728]{2,1,0:T(8,128)} %fusion.94, bf16[16,64,1,128]{3,1,0,2:T(8,128)(2,1)S(1)} %get-tuple-element.237, s32[]{:T(128)S(6)} %select_n.30), kind=kOutput, calls=%fused_computation.16.clone.1 | convolution fusion | flops 232687808 | bytes 18219012 | tf_op jit(solution)/shard_map/while/body/eval_jaxpr/ahij,aihd->ajhd/dot_general | solution.py:87
  238.0 23.2 %scatter_fusion = f32[16,64,128]{2,1,0:T(8,128)S(1)} fusion(f32[16,64,128]{2,1,0:T(8,128)S(1)} %bitcast.162, s32[216]{0:T(256)S(1)} %reshape.617, f32[216,64,128]{2,1,0:T(8,128)} %bitcast.172), kind=kCustom, calls=%fused_computation.2.clone.1 | custom fusion | flops 1769472 | bytes 21234528 | tf_op jit(solution)/shard_map/while/body/eval_jaxpr/scatter-add | solution.py:91
  261.2 5.7 %fusion.96 = f32[8,128,1728]{1,2,0:T(8,128)} fusion(bf16[8,64,1728]{2,1,0:T(8,128)(2,1)} %copy-done.2, bf16[16,64,1,128]{3,1,0,2:T(8,128)(2,1)S(1)} %get-tuple-element.240, s32[]{:T(128)S(6)} %select_n.30), kind=kOutput, calls=%fused_computation.23.clone.1 | convolution fusion | flops 226492416 | bytes 8978436 | tf_op jit(solution)/shard_map/while/body/eval_jaxpr/ahij,aihd->ajhd/dot_general | solution.py:75
  266.9 23.2 %scatter_fusion.1 = f32[16,64,128]{2,1,0:T(8,128)S(1)} fusion(f32[16,64,128]{2,1,0:T(8,128)S(1)} %bitcast.164, s32[216]{0:T(256)S(1)} %reshape.617, f32[216,64,128]{2,1,0:T(8,128)} %bitcast.171), kind=kCustom, calls=%fused_computation.3.clone.1 | custom fusion | flops 1769472 | bytes 21234528 | tf_op jit(solution)/shard_map/while/body/eval_jaxpr/scatter-add | solution.py:92
  293.3 2.2 divide_convert_fusion.1
  295.9 7.1 %convolution_convert_fusion = bf16[1024,3072]{1,0:T(8,128)(2,1)} fusion(bf16[1024,384]{0,1:T(8,128)(2,1)S(1)} %bitcast.183, bf16[1,3072,1,384]{3,1,2,0:T(8,128)(2,1)} %param.13), kind=kOutput, calls=%fused_computation.50 | convolution fusion | flops 2419064832 | bytes 9437184 | tf_op jit(solution)/shard_map/tc,dc->td/dot_general | solution.py:192
  303.9 6.4 %fusion.50 = f32[1024,3072]{1,0:T(8,128)} fusion(bf16[1024,128]{1,0:T(8,128)(2,1)S(1)} %bitcast.186, bf16[1,128,3072]{2,1,0:T(8,128)(2,1)S(1)} %copy-done), kind=kOutput, calls=%fused_computation.63 | convolution fusion | flops 805306368 | bytes 13631488 | tf_op jit(solution)/shard_map/dot_general | solution.py:164
  310.3 58.0 %reduce-scatter.5.cloned.1.call-done = bf16[64,3072]{1,0:T(8,128)(2,1)} async-done(((bf16[1024,3072]{1,0:T(8,128)(2,1)}), bf16[64,3072]{1,0:T(8,128)(2,1)}) %reduce-scatter.5.cloned.1.call-update) | async-done | bytes 393232 | tf_op jit(solution)/shard_map/reduce_scatter | solution.py:191
  368.3 80.7 %reduce-scatter.3.cloned.1.call-done = f32[64,3072]{1,0:T(8,128)} async-done(((f32[1024,3072]{1,0:T(8,128)}), f32[64,3072]{1,0:T(8,128)}) %reduce-scatter.3.cloned.1.call-update) | async-done | bytes 786448 | tf_op jit(solution)/shard_map/reduce_scatter | solution.py:163
  455.1 46.7 %all-reduce = f32[3072]{0:T(1024)S(1)} all-reduce(f32[3072]{0:T(1024)S(1)} %get-tuple-element.116), channel_id=5, replica_groups=mesh['seq'=16,'pipe'=4,'dp'=4] {'seq'}, use_global_device_ids=true, to_apply=%region_17.18.clone | all-reduce | flops 3072 | bytes 24576
  (124 shorter events, 25.4 us)
Async XLA Ops:
  7.2 98.8 %copy-start = (bf16[1,128,3072]{2,1,0:T(8,128)(2,1)S(1)}, bf16[1,128,3072]{2,1,0:T(8,128)(2,1)}, u32[]{:S(2)}) copy-start(bf16[1,128,3072]{2,1,0:T(8,128)(2,1)} %param.14) | copy-start | bytes 2359300
  7.2 5.6 %copy-start.25 = (s32[16]{0:T(128)S(1)}, s32[16]{0:T(128)}, u32[]{:S(2)}) copy-start(s32[16]{0:T(128)} %param.19) | copy-start | bytes 196
  7.2 5.7 %copy-start.20 = (s32[16,27]{1,0:T(8,128)S(1)}, s32[16,27]{1,0:T(8,128)}, u32[]{:S(2)}) copy-start(s32[16,27]{1,0:T(8,128)} %param.18) | copy-start | bytes 5188
  7.2 51.7 %all-gather.6.cloned.1.call-start = ((), (), s32[]{:S(2)}) async-start(), calls=%async_computation.5 | async-start | bytes 6684672 | tf_op jit(solution)/shard_map/all_gather | solution.py:131
  7.9 98.1 %all-gather.4.cloned.1.call-start = ((), (), s32[]{:S(2)}) async-start(), calls=%async_computation.2 | async-start | bytes 6684672 | tf_op jit(solution)/shard_map/all_gather | solution.py:145
  9.8 358.5 %reduce-scatter.5.cloned.1.call-start = ((), (), s32[]{:S(2)}) async-start(), calls=%async_computation.4 | async-start | bytes 6684672 | tf_op jit(solution)/shard_map/reduce_scatter | solution.py:191
  58.9 8.1 %copy-start.21 = (f32[1,128]{1,0:T(1,128)S(1)}, f32[1,128]{1,0:T(1,128)}, u32[]{:S(2)}) copy-start(f32[1,128]{1,0:T(1,128)} %param.15) | copy-start | bytes 1540
  58.9 8.3 %copy-start.23 = (f32[1,128]{1,0:T(1,128)S(1)}, f32[1,128]{1,0:T(1,128)}, u32[]{:S(2)}) copy-start(f32[1,128]{1,0:T(1,128)} %param.16) | copy-start | bytes 1540
  65.9 44.6 %copy-start.3 = (f32[1024,1,1,128]{3,0,2,1:T(8,128)}, f32[1024,1,1,128]{3,0,2,1:T(8,128)S(1)}, u32[]{:S(2)}) copy-start(f32[1024,1,1,128]{3,0,2,1:T(8,128)S(1)} %get-tuple-element.115) | copy-start | bytes 1572868
  66.0 44.6 %copy-start.5 = (f32[1024,1,1,128]{3,0,2,1:T(8,128)}, f32[1024,1,1,128]{3,0,2,1:T(8,128)S(1)}, u32[]{:S(2)}) copy-start(f32[1024,1,1,128]{3,0,2,1:T(8,128)S(1)} %get-tuple-element.114) | copy-start | bytes 1572868
  66.0 44.6 %copy-start.17 = (f32[1024]{0:T(1024)}, f32[1024]{0:T(1024)S(1)}, u32[]{:S(2)}) copy-start(f32[1024]{0:T(1024)S(1)} %get-tuple-element.119) | copy-start | bytes 12292
  67.0 43.6 %copy-start.12 = (f32[16,64]{1,0:T(8,128)}, f32[16,64]{1,0:T(8,128)S(1)}, u32[]{:S(2)}) copy-start(f32[16,64]{1,0:T(8,128)S(1)} %sqrt.31) | copy-start | bytes 12292
  110.7 179.4 %copy-start.13 = (f32[16,64]{1,0:T(8,128)S(1)}, f32[16,64]{1,0:T(8,128)}, u32[]{:S(2)}) copy-start(f32[16,64]{1,0:T(8,128)} %copy-done.12) | copy-start | bytes 12292
  110.7 179.4 %copy-start.24 = (f32[1,128]{1,0:T(1,128)S(1)}, f32[1,128]{1,0:T(1,128)}, u32[]{:S(2)}) copy-start(f32[1,128]{1,0:T(1,128)} %param.16) | copy-start | bytes 1540
  110.7 180.9 %copy-start.4 = (f32[1024,1,1,128]{3,0,2,1:T(8,128)S(1)}, f32[1024,1,1,128]{3,0,2,1:T(8,128)}, u32[]{:S(2)}) copy-start(f32[1024,1,1,128]{3,0,2,1:T(8,128)} %copy-done.3) | copy-start | bytes 1572868
  110.8 180.9 %copy-start.19 = (f32[2,8,64]{2,1,0:T(8,128)S(1)}, f32[2,8,64]{2,1,0:T(8,128)}, u32[]{:S(2)}) copy-start(f32[2,8,64]{2,1,0:T(8,128)} %sqrt.32) | copy-start | bytes 12292
  110.8 180.9 %copy-start.22 = (f32[1,128]{1,0:T(1,128)S(1)}, f32[1,128]{1,0:T(1,128)}, u32[]{:S(2)}) copy-start(f32[1,128]{1,0:T(1,128)} %param.15) | copy-start | bytes 1540
  110.8 182.5 %copy-start.15 = (f32[1024]{0:T(1024)S(1)}, f32[1024]{0:T(1024)}, u32[]{:S(2)}) copy-start(f32[1024]{0:T(1024)} %copy-done.14) | copy-start | bytes 12292
  110.8 182.5 %copy-start.18 = (f32[1024]{0:T(1024)S(1)}, f32[1024]{0:T(1024)}, u32[]{:S(2)}) copy-start(f32[1024]{0:T(1024)} %copy-done.17) | copy-start | bytes 12292
  123.7 4.0 copy-start.1
  123.7 4.0 copy-start.9
  126.5 1.2 copy-start.2
  213.3 4.0 copy-start.1
  213.3 4.0 copy-start.9
  216.1 1.2 copy-start.2
  303.0 146.0 %reduce-scatter.3.cloned.1.call-start = ((), (), s32[]{:S(2)}) async-start(), calls=%async_computation.3 | async-start | bytes 13369344 | tf_op jit(solution)/shard_map/reduce_scatter | solution.py:163
  310.3 138.8 %copy-start.7 = (bf16[1,64,3072]{2,1,0:T(8,128)(2,1)S(1)}, bf16[1,64,3072]{2,1,0:T(8,128)(2,1)}, u32[]{:S(2)}) copy-start(bf16[1,64,3072]{2,1,0:T(8,128)(2,1)} %param.11) | copy-start | bytes 1179652
  310.3 138.8 %copy-start.8 = (bf16[1,64,3072]{2,1,0:T(8,128)(2,1)S(1)}, bf16[1,64,3072]{2,1,0:T(8,128)(2,1)}, u32[]{:S(2)}) copy-start(bf16[1,64,3072]{2,1,0:T(8,128)(2,1)} %param.12) | copy-start | bytes 1179652
  310.3 138.8 %copy-start.16 = (f32[1,3072]{1,0:T(1,128)S(1)}, f32[1,3072]{1,0:T(1,128)}, u32[]{:S(2)}) copy-start(f32[1,3072]{1,0:T(1,128)} %param.17) | copy-start | bytes 36868
  310.3 143.6 %copy-start.26 = (u32[256]{0:T(256)S(1)}, u32[256]{0:T(256)}, u32[]{:S(2)}) copy-start(u32[256]{0:T(256)} %constant.48) | copy-start | bytes 3076
  450.6 51.9 %collective-permute-start = (bf16[64,3072]{1,0:T(8,128)(2,1)S(1)}, bf16[64,3072]{1,0:T(8,128)(2,1)S(1)}, u32[]{:S(2)}, u32[]{:S(2)}) collective-permute-start(bf16[64,3072]{1,0:T(8,128)(2,1)S(1)} %get-tuple-element.117), channel_id=1, source_target_pairs={{12,0},{0,4},{4,8},{8,12},{13,1},{1,5},{5,9},{9,13},{14,2},{2,6},{... | collective-permute-start | bytes 1179656 | tf_op jit(solution)/shard_map/ppermute | solution.py:14
  452.1 50.3 %collective-permute-start.1 = (bf16[64,3072]{1,0:T(8,128)(2,1)S(1)}, bf16[64,3072]{1,0:T(8,128)(2,1)S(1)}, u32[]{:S(2)}, u32[]{:S(2)}) collective-permute-start(bf16[64,3072]{1,0:T(8,128)(2,1)S(1)} %get-tuple-element.118), channel_id=1, source_target_pairs={{4,0},{8,4},{12,8},{0,12},{5,1},{9,5},{13,9},{1,13},{6,2},{10,6},{... | collective-permute-start | bytes 1179656 | tf_op jit(solution)/shard_map/ppermute | solution.py:14
  (5 other events, 4.7 us)
Sparse Core Ops, SparseCore 0:
  9.9 48.9 all-gather.5
  61.3 44.6 all-gather.3
  303.1 65.1 reduce-scatter.4
  370.7 78.2 reduce-scatter.2
where the time goes:
time: 514 us; the launch traced here: 511 us
  waiting for transfers between devices  224 us (44%)
  other arithmetic  108 us (21%)
  matrix products  85.4 us (17%)
  blocking collectives  46.7 us (9%)
  local copies, waits for them, and re-layouts  26.4 us (5%)
  between operations  14.8 us (3%)
    reduce_scatter x1, waiting for transfers between devices, body(): lax.psum_scatter(jnp.dot(rows, out_local, preferred_element_type=jnp.floa...  80.7 us
    reduce_scatter x1, waiting for transfers between devices, body(): lax.psum_scatter(jnp.einsum('tc,dc->td', rows, proj_weight, preferred_ele...  58 us
    unnamed x1, blocking collectives  46.7 us
    scatter-add x2, other arithmetic, per_block(): key_total = key_total.at[block_slots].add(key_part.reshape(block_shape))  46.5 us
    scatter-add x2, other arithmetic, per_block(): value_total.at[block_slots].add(value_part.reshape(block_shape))  46.5 us
    all_gather x1, waiting for transfers between devices, body(): lax.all_gather(stream, 'seq', axis=0, tiled=True)  45.7 us
    all_gather x1, waiting for transfers between devices, body(): lax.all_gather(scaled, 'seq', axis=0, tiled=True)  38.6 us
    dot_general x2, matrix products, per_block(): jnp.einsum('ahij,aihd->ajhd', score_grad, query_block, preferred_element_...  17.5 us
  transfers between devices with their start and end apart: 6, of which 4 were waited for; matrix products, arithmetic and copies ran while one was open for 4% of the time, Pallas kernels for 0%

commit v1 on v0

--- a/solution.py
+++ b/solution.py
@@ -128,7 +128,9 @@
     query_weights = query_gain[0]
     key_weights = key_gain[0]
     projected = jnp.dot(
-        lax.all_gather(stream, "seq", axis=0, tiled=True),
+        jnp.concatenate(
+            lax.all_to_all(jnp.stack([stream] * lax.axis_size("seq")), "seq", 0, 0), axis=0
+        ),
         proj_weight,
         preferred_element_type=jnp.float32,
     )

time: 514 us -> 607 us (1.18)
  waiting for transfers between devices: 224 us -> 302 us
  starting transfers between devices: 3.47 us -> 12.2 us
    all_to_all x0 -> x1, waiting for transfers between devices: none -> 163 us  [body(): lax.all_to_all(jnp.stack([stream] * lax.axis_size('seq')), 'seq', 0, 0)]
    all_gather x1 -> x0, waiting for transfers between devices: 45.7 us -> none  [body(): lax.all_gather(stream, 'seq', axis=0, tiled=True)]
    all_gather x1, waiting for transfers between devices: 38.6 us -> 0.02 us  [body(): lax.all_gather(scaled, 'seq', axis=0, tiled=True)]
    all_to_all x0 -> x1, starting transfers between devices: none -> 8.75 us  [body(): lax.all_to_all(jnp.stack([stream] * lax.axis_size('seq')), 'seq', 0, 0)]
  transfers between devices with their start and end apart: 6 -> 6, of which waited for: 4 -> 3; matrix products, arithmetic and copies ran while one was open for 4% -> 3% of each run, Pallas kernels for 0% -> 0%
where the time goes in v1:
time: 607 us; the launch traced here: 604 us
  waiting for transfers between devices  302 us (50%)
  other arithmetic  107 us (18%)
  matrix products  86.1 us (14%)
  blocking collectives  46.7 us (8%)
  local copies, waits for them, and re-layouts  32.3 us (5%)
  between operations  14.9 us (2%)
  starting transfers between devices  12.2 us (2%)
    all_to_all x1, waiting for transfers between devices, body(): lax.all_to_all(jnp.stack([stream] * lax.axis_size('seq')), 'seq', 0, 0)  163 us
    reduce_scatter x1, waiting for transfers between devices, body(): lax.psum_scatter(jnp.dot(rows, out_local, preferred_element_type=jnp.floa...  80.7 us
    reduce_scatter x1, waiting for transfers between devices, body(): lax.psum_scatter(jnp.einsum('tc,dc->td', rows, proj_weight, preferred_ele...  58.6 us
    unnamed x1, blocking collectives  46.7 us
    scatter-add x2, other arithmetic, per_block(): key_total = key_total.at[block_slots].add(key_part.reshape(block_shape))  46.5 us
    scatter-add x2, other arithmetic, per_block(): value_total.at[block_slots].add(value_part.reshape(block_shape))  46.5 us
    dot_general x2, matrix products, per_block(): jnp.einsum('ahij,aihd->ajhd', score_grad, query_block, preferred_element_...  17.5 us
    dot_general x2, matrix products, per_block(): jnp.einsum('ahij,ajhd->aihd', score_grad, key_rows, preferred_element_typ...  14.2 us
  transfers between devices with their start and end apart: 6, of which 3 were waited for; matrix products, arithmetic and copies ran while one was open for 3% of the time, Pallas kernels for 0%

profile of v1, /device:TPU:2, one launch (start us, length us, event | category | flops | bytes accessed | tf_op | source)
XLA Modules:
  0.0 603.5 jit_solution(16983403864259728617)
XLA Ops:
  7.2 4.5 stack.10
  11.7 8.7 %all-to-all-start = ((bf16[16,64,3072]{2,1,0:T(8,128)(2,1)}), bf16[16,64,3072]{2,1,0:T(8,128)(2,1)}, u32[]{:S(2)}, u32[]{:S(2)}) async-start(bf16[16,64,3072]{2,1,0:T(8,128)(2,1)} %stack.10), calls=%async_computation | async-start | bytes 12582912 | tf_op jit(solution)/shard_map/all_to_all | solution.py:132
  21.4 4.3 copy.22
  26.1 163.0 %all-to-all-done = bf16[16,64,3072]{2,1,0:T(8,128)(2,1)} async-done(((bf16[16,64,3072]{2,1,0:T(8,128)(2,1)}), bf16[16,64,3072]{2,1,0:T(8,128)(2,1)}, u32[]{:S(2)}, u32[]{:S(2)}) %all-to-all-start) | async-done | bytes 6291488 | tf_op jit(solution)/shard_map/all_to_all | solution.py:132
  189.1 6.3 %convolution_bitcast_fusion.1 = f32[1024,1,3,128]{3,0,2,1:T(8,128)S(1)} fusion(bf16[1024,3072,1]{1,0,2:T(8,128)(2,1)} %bitcast.26, bf16[3,128,3072]{2,1,0:T(8,128)(2,1)} %bitcast.177), kind=kOutput, calls=%fused_computation.50 | convolution fusion | flops 2415919104 | bytes 10223616 | tf_op jit(solution)/shard_map/dot_general | solution.py:130
  198.4 4.6 convolution_convert_fusion.1
  203.2 179.4 %while.16 = (s32[]{:T(128)}, f32[16,64,1,128]{3,1,0,2:T(8,128)S(1)}, f32[16,64,1,128]{3,1,0,2:T(8,128)S(1)}, bf16[2,8,64,1,128]{4,2,1,3,0:T(8,128)(2,1)}, f32[2,...) while((s32[]{:T(128)}, ...), condition=%wide.region_11.12_spmd, body=%wide.region_5.11_spmd.sunk | while | flops 1380196096 | bytes 147397712 | solution.py:95
  205.0 2.9 gather_fusion.1
  207.9 2.9 gather_fusion
  210.8 5.3 exponential_reduce_fusion.2
  216.1 2.8 divide_convert_fusion.3
  221.7 3.2 fusion.89
  224.9 7.1 %fusion.93 = f32[2,8,64,1,128]{4,2,1,3,0:T(8,128)} fusion(f32[2,8,64,1,128]{4,2,1,3,0:T(8,128)} %get-tuple-element.218, s32[]{:T(128)S(6)} %copy.34, bf16[8,1728,128]{2,1,0:T(8,128)(2,1)} %bitcast.171, bf16[8,64,1728]{2,1,0:T(8,128)(2,1)} %copy-done.2, f32[8,64,1728]{2,1,0:T(8,128)} %fusion.89), kind=kOutput, calls=%fused_computation.20.clone.1 | convolution fusion | flops 232687808 | bytes 14811140 | tf_op jit(solution)/shard_map/while/body/eval_jaxpr/ahij,ajhd->aihd/dot_general | solution.py:84
  232.0 8.8 %fusion.90 = f32[8,128,1728]{1,2,0:T(8,128)} fusion(bf16[8,64,1728]{2,1,0:T(8,128)(2,1)} %copy-done.2, f32[8,64,1728]{2,1,0:T(8,128)} %fusion.89, bf16[16,64,1,128]{3,1,0,2:T(8,128)(2,1)S(1)} %get-tuple-element.237, s32[]{:T(128)S(6)} %select_n.30), kind=kOutput, calls=%fused_computation.16.clone.1 | convolution fusion | flops 232687808 | bytes 18219012 | tf_op jit(solution)/shard_map/while/body/eval_jaxpr/ahij,aihd->ajhd/dot_general | solution.py:87
  240.8 23.2 %scatter_fusion = f32[16,64,128]{2,1,0:T(8,128)S(1)} fusion(f32[16,64,128]{2,1,0:T(8,128)S(1)} %bitcast.159, s32[216]{0:T(256)S(1)} %reshape.620, f32[216,64,128]{2,1,0:T(8,128)} %bitcast.169), kind=kCustom, calls=%fused_computation.2.clone.1 | custom fusion | flops 1769472 | bytes 21234528 | tf_op jit(solution)/shard_map/while/body/eval_jaxpr/scatter-add | solution.py:91
  264.1 5.7 fusion.91
  269.7 23.2 %scatter_fusion.1 = f32[16,64,128]{2,1,0:T(8,128)S(1)} fusion(f32[16,64,128]{2,1,0:T(8,128)S(1)} %bitcast.161, s32[216]{0:T(256)S(1)} %reshape.620, f32[216,64,128]{2,1,0:T(8,128)} %bitcast.168), kind=kCustom, calls=%fused_computation.3.clone.1 | custom fusion | flops 1769472 | bytes 21234528 | tf_op jit(solution)/shard_map/while/body/eval_jaxpr/scatter-add | solution.py:92
  294.6 2.9 gather_fusion.1
  297.5 2.9 gather_fusion
  300.4 5.3 exponential_reduce_fusion.2
  305.7 2.8 divide_convert_fusion.3
  311.3 3.2 fusion.89
  314.5 7.1 %fusion.93 = f32[2,8,64,1,128]{4,2,1,3,0:T(8,128)} fusion(f32[2,8,64,1,128]{4,2,1,3,0:T(8,128)} %get-tuple-element.218, s32[]{:T(128)S(6)} %copy.34, bf16[8,1728,128]{2,1,0:T(8,128)(2,1)} %bitcast.171, bf16[8,64,1728]{2,1,0:T(8,128)(2,1)} %copy-done.2, f32[8,64,1728]{2,1,0:T(8,128)} %fusion.89), kind=kOutput, calls=%fused_computation.20.clone.1 | convolution fusion | flops 232687808 | bytes 14811140 | tf_op jit(solution)/shard_map/while/body/eval_jaxpr/ahij,ajhd->aihd/dot_general | solution.py:84
  321.6 8.8 %fusion.90 = f32[8,128,1728]{1,2,0:T(8,128)} fusion(bf16[8,64,1728]{2,1,0:T(8,128)(2,1)} %copy-done.2, f32[8,64,1728]{2,1,0:T(8,128)} %fusion.89, bf16[16,64,1,128]{3,1,0,2:T(8,128)(2,1)S(1)} %get-tuple-element.237, s32[]{:T(128)S(6)} %select_n.30), kind=kOutput, calls=%fused_computation.16.clone.1 | convolution fusion | flops 232687808 | bytes 18219012 | tf_op jit(solution)/shard_map/while/body/eval_jaxpr/ahij,aihd->ajhd/dot_general | solution.py:87
  330.4 23.2 %scatter_fusion = f32[16,64,128]{2,1,0:T(8,128)S(1)} fusion(f32[16,64,128]{2,1,0:T(8,128)S(1)} %bitcast.159, s32[216]{0:T(256)S(1)} %reshape.620, f32[216,64,128]{2,1,0:T(8,128)} %bitcast.169), kind=kCustom, calls=%fused_computation.2.clone.1 | custom fusion | flops 1769472 | bytes 21234528 | tf_op jit(solution)/shard_map/while/body/eval_jaxpr/scatter-add | solution.py:91
  353.7 5.7 fusion.91
  359.3 23.2 %scatter_fusion.1 = f32[16,64,128]{2,1,0:T(8,128)S(1)} fusion(f32[16,64,128]{2,1,0:T(8,128)S(1)} %bitcast.161, s32[216]{0:T(256)S(1)} %reshape.620, f32[216,64,128]{2,1,0:T(8,128)} %bitcast.168), kind=kCustom, calls=%fused_computation.3.clone.1 | custom fusion | flops 1769472 | bytes 21234528 | tf_op jit(solution)/shard_map/while/body/eval_jaxpr/scatter-add | solution.py:92
  388.3 7.1 %convolution_convert_fusion = bf16[1024,3072]{1,0:T(8,128)(2,1)} fusion(bf16[1024,384]{0,1:T(8,128)(2,1)S(1)} %bitcast.181, bf16[1,3072,1,384]{3,1,2,0:T(8,128)(2,1)} %param.13), kind=kOutput, calls=%fused_computation.48 | convolution fusion | flops 2419064832 | bytes 9437184 | tf_op jit(solution)/shard_map/tc,dc->td/dot_general | solution.py:194
  396.4 6.4 %fusion.44 = f32[1024,3072]{1,0:T(8,128)} fusion(bf16[1024,128]{1,0:T(8,128)(2,1)S(1)} %bitcast.184, bf16[1,128,3072]{2,1,0:T(8,128)(2,1)S(1)} %copy-done), kind=kOutput, calls=%fused_computation.59 | convolution fusion | flops 805306368 | bytes 13631488 | tf_op jit(solution)/shard_map/dot_general | solution.py:166
  402.7 58.6 %reduce-scatter.5.cloned.1.call-done = bf16[64,3072]{1,0:T(8,128)(2,1)} async-done(((bf16[1024,3072]{1,0:T(8,128)(2,1)}), bf16[64,3072]{1,0:T(8,128)(2,1)}) %reduce-scatter.5.cloned.1.call-update) | async-done | bytes 393232 | tf_op jit(solution)/shard_map/reduce_scatter | solution.py:193
  461.4 80.7 %reduce-scatter.3.cloned.1.call-done = f32[64,3072]{1,0:T(8,128)} async-done(((f32[1024,3072]{1,0:T(8,128)}), f32[64,3072]{1,0:T(8,128)}) %reduce-scatter.3.cloned.1.call-update) | async-done | bytes 786448 | tf_op jit(solution)/shard_map/reduce_scatter | solution.py:165
  548.1 46.7 %all-reduce = f32[3072]{0:T(1024)S(1)} all-reduce(f32[3072]{0:T(1024)S(1)} %get-tuple-element.116), channel_id=4, replica_groups=mesh['seq'=16,'pipe'=4,'dp'=4] {'seq'}, use_global_device_ids=true, to_apply=%region_17.18.clone | all-reduce | flops 3072 | bytes 24576
  (128 shorter events, 25.9 us)
Async XLA Ops:
  7.2 191.2 %copy-start = (bf16[1,128,3072]{2,1,0:T(8,128)(2,1)S(1)}, bf16[1,128,3072]{2,1,0:T(8,128)(2,1)}, u32[]{:S(2)}) copy-start(bf16[1,128,3072]{2,1,0:T(8,128)(2,1)} %param.14) | copy-start | bytes 2359300
  11.7 8.8 %copy-start.8 = (bf16[1,64,3072]{2,1,0:T(8,128)(2,1)S(1)}, bf16[1,64,3072]{2,1,0:T(8,128)(2,1)}, u32[]{:S(2)}) copy-start(bf16[1,64,3072]{2,1,0:T(8,128)(2,1)} %param.12) | copy-start | bytes 1179652
  11.7 8.8 %copy-start.17 = (f32[1,3072]{1,0:T(1,128)S(1)}, f32[1,3072]{1,0:T(1,128)}, u32[]{:S(2)}) copy-start(f32[1,3072]{1,0:T(1,128)} %param.17) | copy-start | bytes 36868
  11.7 177.5 %all-to-all-start = ((bf16[16,64,3072]{2,1,0:T(8,128)(2,1)}), bf16[16,64,3072]{2,1,0:T(8,128)(2,1)}, u32[]{:S(2)}, u32[]{:S(2)}) async-start(bf16[16,64,3072]{2,1,0:T(8,128)(2,1)} %stack.10), calls=%async_computation | async-start | bytes 12582912 | tf_op jit(solution)/shard_map/all_to_all | solution.py:132
  20.4 5.3 copy-start.27
  20.4 5.4 copy-start.22
  20.4 177.9 %all-gather.2.cloned.1.call-start = ((), (), s32[]{:S(2)}) async-start(), calls=%async_computation.3 | async-start | bytes 6684672 | tf_op jit(solution)/shard_map/all_gather | solution.py:147
  21.3 440.0 %reduce-scatter.5.cloned.1.call-start = ((), (), s32[]{:S(2)}) async-start(), calls=%async_computation.5 | async-start | bytes 6684672 | tf_op jit(solution)/shard_map/reduce_scatter | solution.py:193
  189.1 8.8 %copy-start.23 = (f32[1,128]{1,0:T(1,128)S(1)}, f32[1,128]{1,0:T(1,128)}, u32[]{:S(2)}) copy-start(f32[1,128]{1,0:T(1,128)} %param.15) | copy-start | bytes 1540
  189.1 9.0 %copy-start.25 = (f32[1,128]{1,0:T(1,128)S(1)}, f32[1,128]{1,0:T(1,128)}, u32[]{:S(2)}) copy-start(f32[1,128]{1,0:T(1,128)} %param.16) | copy-start | bytes 1540
  196.9 6.0 %copy-start.3 = (f32[1024,1,1,128]{3,0,2,1:T(8,128)}, f32[1024,1,1,128]{3,0,2,1:T(8,128)S(1)}, u32[]{:S(2)}) copy-start(f32[1024,1,1,128]{3,0,2,1:T(8,128)S(1)} %get-tuple-element.115) | copy-start | bytes 1572868
  196.9 6.0 %copy-start.5 = (f32[1024,1,1,128]{3,0,2,1:T(8,128)}, f32[1024,1,1,128]{3,0,2,1:T(8,128)S(1)}, u32[]{:S(2)}) copy-start(f32[1024,1,1,128]{3,0,2,1:T(8,128)S(1)} %get-tuple-element.114) | copy-start | bytes 1572868
  197.0 6.0 copy-start.19
  197.9 5.1 copy-start.13
  203.1 179.5 %copy-start.14 = (f32[16,64]{1,0:T(8,128)S(1)}, f32[16,64]{1,0:T(8,128)}, u32[]{:S(2)}) copy-start(f32[16,64]{1,0:T(8,128)} %copy-done.13) | copy-start | bytes 12292
  203.1 179.5 %copy-start.26 = (f32[1,128]{1,0:T(1,128)S(1)}, f32[1,128]{1,0:T(1,128)}, u32[]{:S(2)}) copy-start(f32[1,128]{1,0:T(1,128)} %param.16) | copy-start | bytes 1540
  203.1 180.9 %copy-start.4 = (f32[1024,1,1,128]{3,0,2,1:T(8,128)S(1)}, f32[1024,1,1,128]{3,0,2,1:T(8,128)}, u32[]{:S(2)}) copy-start(f32[1024,1,1,128]{3,0,2,1:T(8,128)} %copy-done.3) | copy-start | bytes 1572868
  203.2 180.9 %copy-start.21 = (f32[2,8,64]{2,1,0:T(8,128)S(1)}, f32[2,8,64]{2,1,0:T(8,128)}, u32[]{:S(2)}) copy-start(f32[2,8,64]{2,1,0:T(8,128)} %sqrt.32) | copy-start | bytes 12292
  203.2 180.9 %copy-start.24 = (f32[1,128]{1,0:T(1,128)S(1)}, f32[1,128]{1,0:T(1,128)}, u32[]{:S(2)}) copy-start(f32[1,128]{1,0:T(1,128)} %param.15) | copy-start | bytes 1540
  203.2 182.5 %copy-start.16 = (f32[1024]{0:T(1024)S(1)}, f32[1024]{0:T(1024)}, u32[]{:S(2)}) copy-start(f32[1024]{0:T(1024)} %copy-done.15) | copy-start | bytes 12292
  203.2 182.5 %copy-start.20 = (f32[1024]{0:T(1024)S(1)}, f32[1024]{0:T(1024)}, u32[]{:S(2)}) copy-start(f32[1024]{0:T(1024)} %copy-done.19) | copy-start | bytes 12292
  216.1 4.0 copy-start.1
  216.1 4.0 copy-start.10
  305.7 4.0 copy-start.1
  305.7 4.0 copy-start.10
  395.4 146.6 %reduce-scatter.3.cloned.1.call-start = ((), (), s32[]{:S(2)}) async-start(), calls=%async_computation.4 | async-start | bytes 13369344 | tf_op jit(solution)/shard_map/reduce_scatter | solution.py:165
  402.7 139.4 %copy-start.7 = (bf16[1,64,3072]{2,1,0:T(8,128)(2,1)S(1)}, bf16[1,64,3072]{2,1,0:T(8,128)(2,1)}, u32[]{:S(2)}) copy-start(bf16[1,64,3072]{2,1,0:T(8,128)(2,1)} %param.11) | copy-start | bytes 1179652
  402.7 139.4 %copy-start.9 = (bf16[1,64,3072]{2,1,0:T(8,128)(2,1)S(1)}, bf16[1,64,3072]{2,1,0:T(8,128)(2,1)}, u32[]{:S(2)}) copy-start(bf16[1,64,3072]{2,1,0:T(8,128)(2,1)} %param.12) | copy-start | bytes 1179652
  402.7 139.4 %copy-start.18 = (f32[1,3072]{1,0:T(1,128)S(1)}, f32[1,3072]{1,0:T(1,128)}, u32[]{:S(2)}) copy-start(f32[1,3072]{1,0:T(1,128)} %param.17) | copy-start | bytes 36868
  402.7 144.2 %copy-start.28 = (u32[256]{0:T(256)S(1)}, u32[256]{0:T(256)}, u32[]{:S(2)}) copy-start(u32[256]{0:T(256)} %constant.48) | copy-start | bytes 3076
  543.6 51.9 %collective-permute-start = (bf16[64,3072]{1,0:T(8,128)(2,1)S(1)}, bf16[64,3072]{1,0:T(8,128)(2,1)S(1)}, u32[]{:S(2)}, u32[]{:S(2)}) collective-permute-start(bf16[64,3072]{1,0:T(8,128)(2,1)S(1)} %get-tuple-element.117), channel_id=1, source_target_pairs={{12,0},{0,4},{4,8},{8,12},{13,1},{1,5},{5,9},{9,13},{14,2},{2,6},{... | collective-permute-start | bytes 1179656 | tf_op jit(solution)/shard_map/ppermute | solution.py:14
  545.1 50.4 %collective-permute-start.1 = (bf16[64,3072]{1,0:T(8,128)(2,1)S(1)}, bf16[64,3072]{1,0:T(8,128)(2,1)S(1)}, u32[]{:S(2)}, u32[]{:S(2)}) collective-permute-start(bf16[64,3072]{1,0:T(8,128)(2,1)S(1)} %get-tuple-element.118), channel_id=1, source_target_pairs={{4,0},{8,4},{12,8},{0,12},{5,1},{9,5},{13,9},{1,13},{6,2},{10,6},{... | collective-permute-start | bytes 1179656 | tf_op jit(solution)/shard_map/ppermute | solution.py:14
  (7 other events, 7.2 us)
Sparse Core Ops, SparseCore 0:
  23.7 133.6 all-gather.1
  395.6 65.7 reduce-scatter.4
  464.0 78.0 reduce-scatter.2
